TPU v7x, 32 devices: a whole 2x2x4 slice. The times are simulated.
32 devices in a mesh: dp: 8 (over y, x, core), tensor: 4 (over z).
Axes of the slice: x: 2, y: 2, z: 4, core: 2. Of those that a mesh axis runs over, the one named last changes fastest.
Arguments:
- send_order: int32 [32, 32], P(('dp', 'tensor')), may hold values from 0 to 31, each once within a row
- master: float32 [32, 32, 2048], P(('dp', 'tensor')), may hold values from -6 to 6
- first_code: bfloat16 [32, 32, 2048], P(('dp', 'tensor')), may hold values from -1 to 1
- first_scale: float32 [32, 32], P(('dp', 'tensor')), may hold values from 0.1 to 2
- second_code: bfloat16 [32, 32, 2048], P(('dp', 'tensor')), may hold values from 0.049804688 to 1
- second_scale: float32 [32, 32], P(('dp', 'tensor')), may hold values from 0.5 to 20
- grads: bfloat16 [8, 4, 8, 32, 2048], P('dp', 'tensor'), may hold values from -6 to 6
Outputs:
- new_master: float32 [32, 32, 2048], P(('dp', 'tensor'))
- new_first_code: bfloat16 [32, 32, 2048], P(('dp', 'tensor'))
- new_first_scale: float32 [32, 32], P(('dp', 'tensor'))
- new_second_code: bfloat16 [32, 32, 2048], P(('dp', 'tensor'))
- new_second_scale: float32 [32, 32], P(('dp', 'tensor'))
- weights: bfloat16 [4, 8, 32, 2048], P('tensor')
Inputs may be any that keep to these rules, and one draw needn't show every extreme that they name: `send_order`: each row is an ordering of the slots 0 to 31, each once.
All inputs are finite; a program needn't handle non-finite values. Where the computation divides by a largest or mean magnitude, that divisor is 1e-20 or more.
Results may differ from a plain program's by a relative error of at most 0.001.
Values may be sent and summed in bfloat16 or wider, within the bound.
A program may use at most 128 MiB of HBM per device.

v0:
```python
import functools

import jax
import jax.numpy as jnp
from jax import lax
from jax.experimental import pallas as pl
from jax.experimental.pallas import tpu as pltpu
from jax.sharding import PartitionSpec as P

STEP = 10
LANES = 128
RELAYS = 2
PARTS = 4
MESH = pl.DeviceIdType.MESH


def _kernel(nd, nt, slots, width, order_hbm, m_hbm, c1_hbm, s1_hbm, c2_hbm, s2_hbm, g_hbm,
            nm_out, nc1_out, ns1_out, nc2_out, ns2_out, wg,
            order_v, s1_v, s2_v, m_v, c1_v, c2_v,
            xs_m, xs_f, xs_c, xs_s, xr_m, xr_c, xr_s, raw_x, raw_y, out_x, out_y, got_x, got_y, m1_v, m2_v,
            in_sem, rm, rc, rs, rg, sm, sc, ss, sg, rh, sh, ra, sa, rf, sf):
    n = nd * nt
    per = slots // n
    chunks = width // LANES
    cp = chunks // RELAYS
    cq = chunks // PARTS
    wr = width // RELAYS
    wp = width // PARTS
    half_m = slots * cp
    half_c = slots * 2 * cp
    ny = nd // 4
    chips = 2 * ny
    my_dp = lax.axis_index("dp")
    my_t = lax.axis_index("tensor")
    me = my_dp * nt + my_t
    my_c = lax.rem(my_dp, 2)
    my_chip = my_dp // 2
    my_x = lax.rem(my_chip, 2)
    my_y = my_chip // 2
    partner = my_dp + 1 - 2 * my_c

    def dp_of(y, x, c):
        return (y * 2 + x) * 2 + c


    loads = [
        pltpu.make_async_copy(order_hbm, order_v, in_sem.at[0]),
        pltpu.make_async_copy(s1_hbm, s1_v, in_sem.at[1]),
        pltpu.make_async_copy(s2_hbm, s2_v, in_sem.at[2]),
        pltpu.make_async_copy(m_hbm.at[0], m_v, in_sem.at[3]),
        pltpu.make_async_copy(c1_hbm.at[0], c1_v, in_sem.at[4]),
        pltpu.make_async_copy(c2_hbm.at[0], c2_v, in_sem.at[5]),
    ]
    for item in loads:
        item.start()

    barrier = pltpu.get_barrier_semaphore()

    def greet(k, carry):
        dst = lax.rem(me + k, n)
        pl.semaphore_signal(barrier, inc=1, device_id=(dst // nt, lax.rem(dst, nt)), device_id_type=MESH)
        return carry

    lax.fori_loop(1, n, greet, 0)

    def cols(h):
        return pl.ds(h * wp, wp)

    def wide(r):
        return pl.ds(r * wr, wr)

    def slabs(h, y, x, c):
        if h % 2 == 0:
            return g_hbm.at[:, x, c, :, cols(h)]
        return g_hbm.at[y, :, c, :, cols(h)]

    def raw_at(h, y, x, c):
        return raw_x.at[h // 2, x, c] if h % 2 == 0 else raw_y.at[h // 2, y, c]

    for h in range(PARTS):
        pltpu.make_async_copy(slabs(h, my_y, my_x, my_c), raw_at(h, my_y, my_x, my_c), rg.at[h]).start()

    for item in loads:
        item.wait()
    row = lax.broadcasted_iota(jnp.int32, (slots, slots), 0)
    lane = lax.broadcasted_iota(jnp.int32, (slots, slots), 1)
    eye = row == lane
    order_f = order_v[...].astype(jnp.float32)
    order_col = jnp.sum(jnp.where(eye, order_f, 0.0), axis=1, keepdims=True)
    pick = order_col == lane.astype(jnp.float32)
    s1_col = jnp.sum(jnp.where(pick, s1_v[...], 0.0), axis=1, keepdims=True)
    s2_col = jnp.sum(jnp.where(pick, s2_v[...], 0.0), axis=1, keepdims=True)
    side = lax.broadcasted_iota(jnp.int32, (slots, LANES), 1) < LANES // 2
    xs_s[:, 0, :] = jnp.where(side, s1_col, s2_col)
    select = jnp.where(pick, 1.0, 0.0).astype(jnp.bfloat16)

    def take(x):
        return jnp.dot(select, x, preferred_element_type=jnp.float32)

    def stage(h):
        x = m_v[:, wide(h)]
        hi = x.astype(jnp.bfloat16)
        rest = x - hi.astype(jnp.float32)
        mid = rest.astype(jnp.bfloat16)
        low = (rest - mid.astype(jnp.float32)).astype(jnp.bfloat16)
        xm = (take(hi) + take(mid)) + take(low)
        x1 = take(c1_v[:, wide(h)])
        x2 = take(c2_v[:, wide(h)])
        for j in range(cp):
            piece = slice(j * LANES, (j + 1) * LANES)
            xs_m[pl.ds(h * half_m + j, slots, stride=cp), :] = xm[:, piece]
            xs_f[pl.ds(h * half_c + j, slots, stride=2 * cp), :] = x1[:, piece]
            xs_f[pl.ds(h * half_c + cp + j, slots, stride=2 * cp), :] = x2[:, piece]
        xs_c[pl.ds(h * half_c, half_c), :] = xs_f[pl.ds(h * half_c, half_c), :].astype(jnp.bfloat16)

    stage(0)

    pl.semaphore_wait(barrier, n - 1)

    def drain(ref, sem):
        pltpu.make_async_copy(ref, ref, sem).wait()

    def send_grads(h):
        group = 2 if h % 2 == 0 else ny

        def one(k, carry):
            step = lax.rem(k, 2 * group)
            c = lax.rem(my_c + step, 2)
            away = step // 2
            if h % 2 == 0:
                y, x = my_y, lax.rem(my_x + away, 2)
            else:
                y, x = lax.rem(my_y + away, ny), my_x
            pltpu.make_async_remote_copy(
                src_ref=slabs(h, y, x, c), dst_ref=raw_at(h, my_y, my_x, my_c),
                send_sem=sg.at[h], recv_sem=rg.at[h], device_id=(dp_of(y, x, c), my_t), device_id_type=MESH,
            ).start()
            return carry

        lax.fori_loop(2, 2 * group, one, 0)
        one(1, 0)

    def second(h):
        return (out_x, got_x, ny, my_y) if h % 2 == 0 else (out_y, got_y, 2, my_x)

    def hand_on(h):
        k = h // 2
        raw = (raw_x if h % 2 == 0 else raw_y).at[k]
        drain(raw, rg.at[h])
        out, got, size, mine = second(h)
        for t in range(size):
            for i in range(cq):
                at = slice(i * LANES, (i + 1) * LANES)
                terms = [raw[u, c, t, :, at].astype(jnp.float32) for u in range(raw.shape[0]) for c in range(2)]
                out[k, t, :, at] = functools.reduce(jnp.add, terms)

        def one(away, carry):
            t = lax.rem(mine + away, size)
            where = dp_of(t, my_x, my_c) if h % 2 == 0 else dp_of(my_y, t, my_c)
            pltpu.make_async_remote_copy(
                src_ref=out.at[k, t], dst_ref=got.at[k, mine],
                send_sem=sh.at[h], recv_sem=rh.at[h], device_id=(where, my_t), device_id_type=MESH,
            ).start()
            return carry

        lax.fori_loop(1, size, one, 0)

    bm = per * cp
    bc = per * 2 * cp
    bs = per

    def send_blocks(h):
        def one(k, carry):
            dst = lax.rem(me + k, n)
            where = (dst // nt, lax.rem(dst, nt))
            pltpu.make_async_remote_copy(
                src_ref=xs_m.at[pl.ds(pl.multiple_of(h * half_m + dst * bm, 8), bm)],
                dst_ref=xr_m.at[pl.ds(pl.multiple_of(h * half_m + me * bm, 8), bm)],
                send_sem=sm.at[h], recv_sem=rm.at[h], device_id=where, device_id_type=MESH,
            ).start()
            pltpu.make_async_remote_copy(
                src_ref=xs_c.at[pl.ds(pl.multiple_of(h * half_c + dst * bc, 16), bc)],
                dst_ref=xr_c.at[pl.ds(pl.multiple_of(h * half_c + me * bc, 16), bc)],
                send_sem=sc.at[h], recv_sem=rc.at[h], device_id=where, device_id_type=MESH,
            ).start()
            if h == 0:
                pltpu.make_async_remote_copy(
                    src_ref=xs_s.at[pl.ds(dst * bs, bs)],
                    dst_ref=xr_s.at[pl.ds(me * bs, bs)],
                    send_sem=ss.at[0], recv_sem=rs.at[0], device_id=where, device_id_type=MESH,
                ).start()
            return carry

        lax.fori_loop(1, n, one, 0)
        at_m = pl.ds(pl.multiple_of(h * half_m + me * bm, 8), bm)
        at_c = pl.ds(pl.multiple_of(h * half_c + me * bc, 16), bc)
        pltpu.make_async_copy(xs_m.at[at_m], xr_m.at[at_m], rm.at[h]).start()
        pltpu.make_async_copy(xs_c.at[at_c], xr_c.at[at_c], rc.at[h]).start()
        if h == 0:
            at_s = pl.ds(me * bs, bs)
            pltpu.make_async_copy(xs_s.at[at_s], xr_s.at[at_s], rs.at[0]).start()

    for h in range(PARTS):
        send_grads(h)
    send_blocks(0)
    for r in range(1, RELAYS):
        stage(r)
        send_blocks(r)

    for h in range(PARTS):
        hand_on(h)

    inv_one = 1.0 / (1.0 - 0.9**STEP)
    inv_two = 1.0 / (1.0 - 0.95**STEP)

    def adam(h, s1, s2, tops):
        if h * RELAYS % PARTS == 0:
            r = h * RELAYS // PARTS
            drain(xr_m.at[pl.ds(r * half_m, half_m)], rm.at[r])
            drain(xr_c.at[pl.ds(r * half_c, half_c)], rc.at[r])
            xs_f[pl.ds(r * half_c, half_c), :] = xr_c[pl.ds(r * half_c, half_c), :].astype(jnp.float32)
        out, got, size, mine = second(h)
        k = h // 2
        drain(got.at[k, pl.ds(0, size - 1)], rh.at[h])
        top1, top2 = tops
        for i in range(h * cq, (h + 1) * cq):
            at = slice(i * LANES, (i + 1) * LANES)
            r, j = i // cp, i % cp
            near = slice((i - h * cq) * LANES, (i - h * cq + 1) * LANES)
            grad = out[k, mine, :, near]
            for away in range(1, size):
                grad = grad + got[k, lax.rem(mine + away, size), :, near]
            first = xs_f[pl.ds(r * half_c + j, slots, stride=2 * cp), :] * s1
            other = xs_f[pl.ds(r * half_c + cp + j, slots, stride=2 * cp), :] * s2
            old = xr_m[pl.ds(r * half_m + j, slots, stride=cp), :]
            one = 0.9 * first + 0.1 * grad
            two = 0.95 * other + 0.05 * grad * grad
            update = (one * inv_one) / (jnp.sqrt(two * inv_two) + 1e-08) + 0.1 * old
            new = old - 0.01 * update
            nm_out[0, :, at] = new
            wg[0, my_dp, :, at] = new.astype(jnp.bfloat16)
            m1_v[:, at] = one
            m2_v[:, at] = two
            top1 = jnp.maximum(top1, jnp.abs(one))
            top2 = jnp.maximum(top2, jnp.abs(two))
        return top1, top2

    def gathered(chip, c, h):
        return wg.at[0, chip * 2 + c, :, cols(h)]

    def to_chip(h, chip, y, x):
        slab = gathered(chip, my_c, h)
        return pltpu.make_async_remote_copy(
            src_ref=slab, dst_ref=slab, send_sem=sa.at[h], recv_sem=ra.at[h, chip],
            device_id=(dp_of(y, x, my_c), my_t), device_id_type=MESH,
        )

    def to_partner(h, chip):
        slab = gathered(chip, my_c, h)
        return pltpu.make_async_remote_copy(
            src_ref=slab, dst_ref=slab, send_sem=sf.at[h], recv_sem=rf.at[h],
            device_id=(partner, my_t), device_id_type=MESH,
        )

    def arrived(h, chip):
        slab = gathered(chip, my_c, h)
        pltpu.make_async_copy(slab, slab, ra.at[h, chip]).wait()
        to_partner(h, chip).start()

    across = 1 - my_x
    rows_away = [lax.rem(my_y + away, ny) for away in range(1, ny)]

    def spread(h):
        to_chip(h, my_chip, my_y, across).start()
        for y in rows_away:
            to_chip(h, my_chip, y, my_x).start()
            to_chip(h, my_chip, y, across).start()
        to_partner(h, my_chip).start()

    def relay(h):
        arrived(h, my_y * 2 + across)
        for y in rows_away:
            arrived(h, y * 2 + my_x)

    def finish(h):
        for y in rows_away:
            arrived(h, y * 2 + across)

    drain(xr_s, rs.at[0])
    scales = xr_s[:, 0, :]
    s1 = scales[:, 0:1]
    s2 = scales[:, LANES // 2:LANES // 2 + 1]
    zero = jnp.zeros((slots, LANES), jnp.float32)
    tops = (zero, zero)
    for h in range(PARTS):
        tops = adam(h, s1, s2, tops)
        spread(h)
    for h in range(PARTS - 1):
        relay(h)

    top1 = jnp.max(tops[0], axis=1, keepdims=True) + 1e-06
    top2 = jnp.max(tops[1], axis=1, keepdims=True) + 1e-06
    ns1_out[...] = jnp.sum(jnp.where(eye, top1, 0.0), axis=0, keepdims=True)
    ns2_out[...] = jnp.sum(jnp.where(eye, top2, 0.0), axis=0, keepdims=True)
    inv1 = 1.0 / top1
    inv2 = 1.0 / top2
    for j in range(chunks):
        at = slice(j * LANES, (j + 1) * LANES)
        nc1_out[0, :, at] = (m1_v[:, at] * inv1).astype(jnp.bfloat16)
        nc2_out[0, :, at] = (m2_v[:, at] * inv2).astype(jnp.bfloat16)

    relay(PARTS - 1)
    for h in range(PARTS):
        finish(h)
    for h in range(PARTS):
        out, got, size, mine = second(h)
        k = h // 2
        theirs = wg.at[0, pl.ds(0, chips), :, cols(h)]
        drain(theirs, rf.at[h])
        drain(theirs, sf.at[h])
        drain(wg.at[0, pl.ds(0, chips - 1), :, cols(h)], sa.at[h])
        drain(got.at[k, pl.ds(0, size - 1)], sh.at[h])
        group = 2 if h % 2 == 0 else ny
        drain(wg.at[0, pl.ds(0, (2 * group - 1) * (nd // (2 * group))), :, cols(h)], sg.at[h])
    for r in range(RELAYS):
        drain(xs_m.at[pl.ds(0, half_m - bm)], sm.at[r])
        drain(xs_c.at[pl.ds(0, half_c - bc)], sc.at[r])
    drain(xs_s.at[pl.ds(0, slots - bs)], ss.at[0])


def _write_out(*refs):
    sem = refs[-1]
    count = (len(refs) - 1) // 2
    copies = [pltpu.make_async_copy(refs[i], refs[count + i], sem.at[i]) for i in range(count)]
    for item in copies:
        item.start()
    for item in copies:
        item.wait()


def on_device(send_order, master, first_code, first_scale, second_code, second_scale, grads):
    arrays = (send_order, master, first_code, first_scale, second_code, second_scale, grads)
    nd = lax.axis_size("dp")
    nt = lax.axis_size("tensor")
    slots = master.shape[1]
    width = master.shape[2]
    f32, b16 = jnp.float32, jnp.bfloat16
    rows = slots * width // LANES
    dma = pltpu.SemaphoreType.DMA
    ny = nd // 4
    pairs = PARTS // 2
    wp = width // PARTS
    arrays = arrays[:6] + (grads.reshape(ny, 2, 2, slots, width),)
    grant = slots * width * (40 + 6 * nd) + slots * 4096 + 6 * 1024 * 1024
    results = (
        ((1, slots, width), f32),
        ((1, slots, width), b16),
        ((1, slots), f32),
        ((1, slots, width), b16),
        ((1, slots), f32),
        ((1, nd, slots, width), b16),
    )
    held = pl.pallas_call(
        functools.partial(_kernel, nd, nt, slots, width),
        out_shape=tuple(pltpu.VMEM(*item) for item in results),
        in_specs=[pl.BlockSpec(memory_space=pltpu.HBM)] * 7,
        out_specs=[pl.BlockSpec(memory_space=pltpu.VMEM)] * 6,
        scratch_shapes=[
            pltpu.VMEM((1, slots), jnp.int32),
            pltpu.VMEM((1, slots), f32),
            pltpu.VMEM((1, slots), f32),
            pltpu.VMEM((slots, width), f32),
            pltpu.VMEM((slots, width), b16),
            pltpu.VMEM((slots, width), b16),
            pltpu.VMEM((rows, LANES), f32),
            pltpu.VMEM((2 * rows, LANES), f32),
            pltpu.VMEM((2 * rows, LANES), b16),
            pltpu.VMEM((slots, 1, LANES), f32),
            pltpu.VMEM((rows, LANES), f32),
            pltpu.VMEM((2 * rows, LANES), b16),
            pltpu.VMEM((slots, 1, LANES), f32),
            pltpu.VMEM((pairs, 2, 2, ny, slots, wp), b16),
            pltpu.VMEM((pairs, ny, 2, 2, slots, wp), b16),
            pltpu.VMEM((pairs, ny, slots, wp), f32),
            pltpu.VMEM((pairs, 2, slots, wp), f32),
            pltpu.VMEM((pairs, ny, slots, wp), f32),
            pltpu.VMEM((pairs, 2, slots, wp), f32),
            pltpu.VMEM((slots, width), f32),
            pltpu.VMEM((slots, width), f32),
            dma((6,)),
            dma((RELAYS,)), dma((RELAYS,)), dma((1,)), dma((PARTS,)),
            dma((RELAYS,)), dma((RELAYS,)), dma((1,)), dma((PARTS,)),
            dma((PARTS,)), dma((PARTS,)),
            dma((PARTS, 2 * ny)), dma((PARTS,)), dma((PARTS,)), dma((PARTS,)),
        ],
        compiler_params=pltpu.CompilerParams(collective_id=0, has_side_effects=True, vmem_limit_bytes=grant),
        name="relayout_adam",
    )(*(pltpu.with_memory_space_constraint(item, pltpu.HBM) for item in arrays))
    return pl.pallas_call(
        _write_out,
        out_shape=tuple(jax.ShapeDtypeStruct(*item) for item in results),
        in_specs=[pl.BlockSpec(memory_space=pltpu.VMEM)] * len(results),
        out_specs=[pl.BlockSpec(memory_space=pltpu.HBM)] * len(results),
        scratch_shapes=[dma((len(results),))],
        compiler_params=pltpu.CompilerParams(vmem_limit_bytes=2 * 1024 * 1024),
        name="write_out",
    )(*(pltpu.with_memory_space_constraint(item, pltpu.VMEM) for item in held))


def solution(mesh):
    placed = (
        P(("dp", "tensor"), None),
        P(("dp", "tensor"), None, None),
        P(("dp", "tensor"), None, None),
        P(("dp", "tensor"), None),
        P(("dp", "tensor"), None, None),
        P(("dp", "tensor"), None),
        P("dp", "tensor", None, None, None),
    )
    return jax.shard_map(
        on_device,
        mesh=mesh,
        in_specs=placed,
        out_specs=(
            P(("dp", "tensor"), None, None),
            P(("dp", "tensor"), None, None),
            P(("dp", "tensor"), None),
            P(("dp", "tensor"), None, None),
            P(("dp", "tensor"), None),
            P("tensor", None, None, None),
        ),
        check_vma=False,
    )
```

profile of v0, /device:TPU:0, one launch (start us, length us, event | category | flops | bytes accessed | tf_op | source)
XLA Modules:
  0.0 33.1 jit_solution(9660719944342128534)
XLA Ops:
  0.6 31.3 %relayout_adam.1 = (f32[1,32,2048]{2,1,0:T(8,128)S(1)}, bf16[1,32,2048]{2,1,0:T(8,128)(2,1)S(1)}, f32[1,32]{1,0:T(1,128)S(1)}, bf16[1,32,2048]{2,1,0:T(8,128)(2,...) custom-call(s32[1,32]{1,0:T(1,128)} %order_hbm.1, f32[1,32,2048]{2,1,0:T(8,128)} %m_hbm.1, ...), custom_call_target="tpu_custom_call" | custom-call | tf_op jit(solution)/shard_map/relayout_adam/pallas_call | solution.py:363
  31.9 1.2 %write_out.1 = (f32[1,32,2048]{2,1,0:T(8,128)}, bf16[1,32,2048]{2,1,0:T(8,128)(2,1)}, f32[1,32]{1,0:T(1,128)}, bf16[1,32,2048]{2,1,0:T(8,128)(2,1)}, f32[1,32]{1,0:T(1,128)}, /*index=5*/bf16[1,8,32,2048]{3,2,1,0:T(8,128)(2,1)}) custom-call(f32[1,32,2048]{2,1,0:T(8,128)S(1)} %get-tuple-element.12.refs_0_, bf16[1,32,2048]{2,1,0:T(8,128)(2,1)S(1)} %get-tuple-element.13.refs_1_, ...), custom_call_target="tpu_custom_call" | custom-call | tf_op jit(solution)/shard_map/write_out/pallas_call | solution.py:399
where the time goes:
time: 33.3 us; the launch traced here: 33.1 us
  Pallas kernels  32.5 us (98%)
  between operations  0.64 us (2%)
    pallas_call x1, Pallas kernels, on_device(): pl.pallas_call(functools.partial(_kernel, nd, nt, slots, width), out_shap...  31.3 us
    pallas_call x1, Pallas kernels, on_device(): pl.pallas_call(_write_out, out_shape=tuple((jax.ShapeDtypeStruct(*item) f...  1.21 us

commit v1 on v0

v1 whole, which is shorter than its diff:
```python
from contextlib import nullcontext as span
import functools
import math

import jax
import jax.numpy as jnp
from jax import lax
from jax.experimental import pallas as pl
from jax.experimental.pallas import tpu as pltpu
from jax.sharding import PartitionSpec as P

STEP = 10
LANES = 128
RELAYS = 2
PARTS = 4
LEVELS = 32767.0
TINY = 1e-30
MESH = pl.DeviceIdType.MESH


def _kernel(nd, nt, slots, width, order_hbm, m_hbm, c1_hbm, s1_hbm, c2_hbm, s2_hbm, g_hbm,
            nm_out, nc1_out, ns1_out, nc2_out, ns2_out, wg,
            order_v, s1_v, s2_v, m_v, c1_v, c2_v, xf_m, xf_c,
            xs_m, xs_c, xs_s, xr_m, xr_c, xr_s, own, got,
            keep_x, keep_y, q1_x, q1_y, r1_x, r1_y, q2_x, q2_y, r2_x, r2_y,
            t1_x, t1_y, u1_x, u1_y, t2_x, t2_y, u2_x, u2_y, m1_v, m2_v,
            in_sem, own_sem, rm, rc, rs, sm, sc, ss, rp, sp,
            ra1, sa1, rb1, sb1, ra2, sa2, rb2, sb2, ra, sa, rf, sf):
    n = nd * nt
    per = slots // n
    chunks = width // LANES
    cp = chunks // RELAYS
    cq = chunks // PARTS
    wr = width // RELAYS
    wp = width // PARTS
    ny = nd // 4
    chips = 2 * ny
    my_dp = lax.axis_index("dp")
    my_t = lax.axis_index("tensor")
    me = my_dp * nt + my_t
    my_c = lax.rem(my_dp, 2)
    my_chip = my_dp // 2
    my_x = lax.rem(my_chip, 2)
    my_y = my_chip // 2
    other_c = 1 - my_c
    other_x = 1 - my_x
    partner = my_dp + 1 - 2 * my_c

    def dp_of(y, x, c):
        return (y * 2 + x) * 2 + c

    def row_away(away):
        return lax.rem(my_y + away, ny)

    barrier = pltpu.get_barrier_semaphore()

    def greet(k, carry):
        dst = lax.rem(me + n - k, n)
        pl.semaphore_signal(barrier, inc=1, device_id=(dst // nt, lax.rem(dst, nt)), device_id_type=MESH)
        return carry

    lax.fori_loop(1, n, greet, 0)

    loads = [
        pltpu.make_async_copy(order_hbm, order_v, in_sem.at[0]),
        pltpu.make_async_copy(m_hbm.at[0], m_v, in_sem.at[3]),
        pltpu.make_async_copy(s1_hbm, s1_v, in_sem.at[1]),
        pltpu.make_async_copy(s2_hbm, s2_v, in_sem.at[2]),
        pltpu.make_async_copy(c1_hbm.at[0], c1_v, in_sem.at[4]),
        pltpu.make_async_copy(c2_hbm.at[0], c2_v, in_sem.at[5]),
    ]
    for item in loads:
        item.start()

    load_own = pltpu.make_async_copy(g_hbm.at[:, :, my_c], own, own_sem.at[0])
    load_own.start()

    def cols(h):
        return pl.ds(h * wp, wp)

    def wide(r):
        return pl.ds(r * wr, wr)

    def drain(ref, sem):
        pltpu.make_async_copy(ref, ref, sem).wait()

    with span("loads"):
        for item in loads:
            item.wait()

    eye = lax.broadcasted_iota(jnp.int32, (slots, slots), 0) == lax.broadcasted_iota(jnp.int32, (slots, slots), 1)

    def as_row(col):
        return jnp.sum(jnp.where(eye, col, 0.0), axis=0, keepdims=True)

    def as_col(row):
        return jnp.sum(jnp.where(eye, row, 0.0), axis=1, keepdims=True)

    def scale_of(x):
        return (jnp.max(jnp.abs(x), axis=1, keepdims=True) + TINY) * (1.0 / LEVELS)

    with span("prep"):
        lane = lax.broadcasted_iota(jnp.int32, (slots, slots), 1)
        order_col = as_col(order_v[...].astype(jnp.float32))
        pick = order_col == lane.astype(jnp.float32)

        def picked(row):
            return jnp.sum(jnp.where(pick, row, 0.0), axis=1, keepdims=True)

        m_scale = scale_of(m_v[...])
        m_inv = 1.0 / m_scale
        place = lax.broadcasted_iota(jnp.int32, (slots, LANES), 1)
        both = jnp.where(place < LANES // 4, picked(s1_v[...]), picked(s2_v[...]))
        xs_s[:, 0, :] = jnp.where(place < LANES // 2, both, picked(as_row(m_scale)))
        select = jnp.where(pick, 1.0, 0.0).astype(jnp.bfloat16)

    def take(x):
        return jnp.dot(select, x, preferred_element_type=jnp.float32)

    def stage(r):
        level = jnp.round(m_v[:, wide(r)] * m_inv)
        high = jnp.round(level * (1.0 / 256.0))
        low = level - 256.0 * high
        xm = 256.0 * take(high.astype(jnp.bfloat16)) + take(low.astype(jnp.bfloat16))
        x1 = take(c1_v[:, wide(r)])
        x2 = take(c2_v[:, wide(r)])
        for j in range(cp):
            piece = slice(j * LANES, (j + 1) * LANES)
            xf_m[r, pl.ds(j, slots, stride=cp), :] = xm[:, piece]
            xf_c[r, pl.ds(j, slots, stride=2 * cp), :] = x1[:, piece]
            xf_c[r, pl.ds(cp + j, slots, stride=2 * cp), :] = x2[:, piece]
        xs_m[r] = xf_m[r].reshape(slots, cp, LANES).astype(jnp.int16)
        xs_c[r] = xf_c[r].reshape(slots, 2 * cp, LANES).astype(jnp.bfloat16)

    with span("stage"):
        for r in range(RELAYS):
            stage(r)

    with span("barrier"):
        pl.semaphore_wait(barrier, n - 1)

    def send_pairs(h):
        pltpu.make_async_remote_copy(
            src_ref=g_hbm.at[:, :, other_c, :, cols(h)], dst_ref=got.at[h],
            send_sem=sp.at[h], recv_sem=rp.at[h], device_id=(partner, my_t), device_id_type=MESH,
        ).start()

    def send_blocks(r):
        for i in range(nt):
            t = i // 2 if i % 2 == 0 else nt - 1 - i // 2

            def one(k, carry, t=t):
                dp = lax.rem(my_dp + k, nd)
                dst = dp * nt + t
                theirs, mine = pl.ds(dst * per, per), pl.ds(me * per, per)
                where = (dp, t)
                pltpu.make_async_remote_copy(
                    src_ref=xs_m.at[r, theirs], dst_ref=xr_m.at[r, mine],
                    send_sem=sm.at[r], recv_sem=rm.at[r], device_id=where, device_id_type=MESH,
                ).start()
                pltpu.make_async_remote_copy(
                    src_ref=xs_c.at[r, theirs], dst_ref=xr_c.at[r, mine],
                    send_sem=sc.at[r], recv_sem=rc.at[r], device_id=where, device_id_type=MESH,
                ).start()
                if r == 0:
                    pltpu.make_async_remote_copy(
                        src_ref=xs_s.at[theirs], dst_ref=xr_s.at[mine],
                        send_sem=ss.at[0], recv_sem=rs.at[0], device_id=where, device_id_type=MESH,
                    ).start()
                return carry

            lax.fori_loop(jnp.where(my_t == t, 1, 0), nd, one, 0)
        mine = pl.ds(me * per, per)
        pltpu.make_async_copy(xs_m.at[r, mine], xr_m.at[r, mine], rm.at[r]).start()
        pltpu.make_async_copy(xs_c.at[r, mine], xr_c.at[r, mine], rc.at[r]).start()
        if r == 0:
            pltpu.make_async_copy(xs_s.at[mine], xr_s.at[mine], rs.at[0]).start()

    def setup(h):
        k = h // 2
        if h % 2 == 0:
            return (keep_x.at[k], q1_x.at[k], r1_x.at[k], t1_x.at[k], u1_x.at[k],
                    q2_x.at[k], r2_x.at[k], t2_x.at[k], u2_x.at[k], my_y)
        return (keep_y.at[k], q1_y.at[k], r1_y.at[k], t1_y.at[k], u1_y.at[k],
                q2_y.at[k], r2_y.at[k], t2_y.at[k], u2_y.at[k], my_x)

    def at_first(h, a):
        return (my_y, other_x) if h % 2 == 0 else (row_away(a + 1), my_x)

    def at_second(h, b):
        return (row_away(b + 1), my_x) if h % 2 == 0 else (my_y, other_x)

    def slab(h, first, t):
        y, x = first
        return (t, x) if h % 2 == 0 else (y, t)

    def pair_sum(h, y, x):
        return own[y, x, :, cols(h)].astype(jnp.float32) + got[h, y, x].astype(jnp.float32)

    def pack(v, q, t):
        scale = scale_of(v)
        q[...] = jnp.round(v * (1.0 / scale)).astype(jnp.int16)
        t[:, :slots] = as_row(scale)

    def unpack(r, u):
        return r[...].astype(jnp.float32) * as_col(u[:, :slots])

    def remote(src, dst, send, recv, place):
        y, x = place
        pltpu.make_async_remote_copy(
            src_ref=src, dst_ref=dst, send_sem=send, recv_sem=recv,
            device_id=(dp_of(y, x, my_c), my_t), device_id_type=MESH,
        ).start()

    def first_stop(h):
        keep, q1, r1, t1, u1 = setup(h)[:5]
        with span(f"waitpair{h}"):
            drain(got.at[h], rp.at[h])
        for a in range(q1.shape[0]):
            place = at_first(h, a)
            for t in range(q1.shape[1]):
                pack(pair_sum(h, *slab(h, place, t)), q1.at[a, t], t1.at[a, t])
            remote(q1.at[a], r1.at[a], sa1.at[h], ra1.at[h], place)
            remote(t1.at[a], u1.at[a], sb1.at[h], rb1.at[h], place)
        for t in range(q1.shape[1]):
            keep[t] = pair_sum(h, *slab(h, (my_y, my_x), t))

    def second_stop(h):
        keep, q1, r1, t1, u1, q2, r2, t2, u2, mine = setup(h)
        with span(f"waitfirst{h}"):
            drain(r1, ra1.at[h])
            drain(u1, rb1.at[h])

        def total(t):
            return functools.reduce(jnp.add, [unpack(r1.at[a, t], u1.at[a, t]) for a in range(r1.shape[0])], keep[t])

        for b in range(q2.shape[0]):
            y, x = at_second(h, b)
            pack(total(y if h % 2 == 0 else x), q2.at[b], t2.at[b])
            remote(q2.at[b], r2.at[b], sa2.at[h], ra2.at[h], (y, x))
            remote(t2.at[b], u2.at[b], sb2.at[h], rb2.at[h], (y, x))
        keep[mine] = total(mine)

    with span("sendpairs"):
        for h in range(PARTS):
            send_pairs(h)
    with span("sendblocks0"):
        send_blocks(0)
    load_own.wait()
    for h in range(PARTS):
        with span(f"first{h}"):
            first_stop(h)
    with span("sendblocks1"):
        for r in range(1, RELAYS):
            send_blocks(r)
    for h in range(PARTS):
        with span(f"second{h}"):
            second_stop(h)

    inv_one = 1.0 / (1.0 - 0.9**STEP)
    inv_two = 1.0 / (1.0 - 0.95**STEP)

    def adam(h, s1, s2, s0, tops):
        if h * RELAYS % PARTS == 0:
            r = h * RELAYS // PARTS
            with span(f"waitblocks{r}"):
                drain(xr_m.at[r], rm.at[r])
                drain(xr_c.at[r], rc.at[r])
            xf_m[r] = xr_m[r].astype(jnp.float32).reshape(slots * cp, LANES)
            xf_c[r] = xr_c[r].astype(jnp.float32).reshape(slots * 2 * cp, LANES)
        keep, q1, r1, t1, u1, q2, r2, t2, u2, mine = setup(h)
        with span(f"waitsecond{h}"):
            drain(r2, ra2.at[h])
            drain(u2, rb2.at[h])
        top1, top2 = tops
        more = [as_col(u2[b, :, :slots]) for b in range(r2.shape[0])]
        for i in range(h * cq, (h + 1) * cq):
            at = slice(i * LANES, (i + 1) * LANES)
            r, j = i // cp, i % cp
            near = slice((i - h * cq) * LANES, (i - h * cq + 1) * LANES)
            grad = keep[mine, :, near]
            for b in range(r2.shape[0]):
                grad = grad + r2[b, :, near].astype(jnp.float32) * more[b]
            first = xf_c[r, pl.ds(j, slots, stride=2 * cp), :] * s1
            other = xf_c[r, pl.ds(cp + j, slots, stride=2 * cp), :] * s2
            old = xf_m[r, pl.ds(j, slots, stride=cp), :] * s0
            one = 0.9 * first + 0.1 * grad
            two = 0.95 * other + 0.05 * grad * grad
            update = (one * inv_one) / (jnp.sqrt(two * inv_two) + 1e-08) + 0.1 * old
            new = old - 0.01 * update
            nm_out[0, :, at] = new
            wg[0, my_dp, :, at] = new.astype(jnp.bfloat16)
            m1_v[:, at] = one
            m2_v[:, at] = two
            top1 = jnp.maximum(top1, jnp.abs(one))
            top2 = jnp.maximum(top2, jnp.abs(two))
        return top1, top2

    def gathered(chip, h):
        return wg.at[0, chip * 2 + my_c, :, cols(h)]

    def to_chip(h, chip, y, x):
        item = gathered(chip, h)
        pltpu.make_async_remote_copy(
            src_ref=item, dst_ref=item, send_sem=sa.at[h], recv_sem=ra.at[h, chip],
            device_id=(dp_of(y, x, my_c), my_t), device_id_type=MESH,
        ).start()

    def to_partner(h, chip):
        item = gathered(chip, h)
        pltpu.make_async_remote_copy(
            src_ref=item, dst_ref=item, send_sem=sf.at[h], recv_sem=rf.at[h],
            device_id=(partner, my_t), device_id_type=MESH,
        ).start()

    def arrived(h, chip):
        item = gathered(chip, h)
        pltpu.make_async_copy(item, item, ra.at[h, chip]).wait()

    rows_away = [row_away(away) for away in range(1, ny)]

    def spread(h):
        to_chip(h, my_chip, my_y, other_x)
        for y in rows_away:
            to_chip(h, my_chip, y, my_x)
        to_partner(h, my_chip)

    def relay(h):
        if h % 2 == 0:
            for y in rows_away:
                chip = y * 2 + my_x
                arrived(h, chip)
                to_chip(h, chip, my_y, other_x)
                to_partner(h, chip)
        else:
            chip = my_y * 2 + other_x
            arrived(h, chip)
            for y in rows_away:
                to_chip(h, chip, y, my_x)
            to_partner(h, chip)

    def finish(h):
        if h % 2 == 0:
            late = [my_y * 2 + other_x]
        else:
            late = [y * 2 + my_x for y in rows_away]
        for chip in late + [y * 2 + other_x for y in rows_away]:
            arrived(h, chip)
            to_partner(h, chip)

    with span("waitscales"):
        drain(xr_s, rs.at[0])
    scales = xr_s[:, 0, :]
    s1 = scales[:, 0:1]
    s2 = scales[:, LANES // 4:LANES // 4 + 1]
    s0 = scales[:, LANES // 2:LANES // 2 + 1]
    zero = jnp.zeros((slots, LANES), jnp.float32)
    tops = (zero, zero)
    for h in range(PARTS):
        with span(f"adam{h}"):
            tops = adam(h, s1, s2, s0, tops)
        with span(f"spread{h}"):
            spread(h)
        if h == PARTS // 2:
            for e in range(PARTS // 2):
                with span(f"relay{e}"):
                    relay(e)
    with span("relay2"):
        for h in range(PARTS // 2, PARTS - 1):
            relay(h)

    with span("codes"):
        top1 = jnp.max(tops[0], axis=1, keepdims=True) + 1e-06
        top2 = jnp.max(tops[1], axis=1, keepdims=True) + 1e-06
        ns1_out[...] = as_row(top1)
        ns2_out[...] = as_row(top2)
        inv1 = 1.0 / top1
        inv2 = 1.0 / top2
        for j in range(chunks):
            at = slice(j * LANES, (j + 1) * LANES)
            nc1_out[0, :, at] = (m1_v[:, at] * inv1).astype(jnp.bfloat16)
            nc2_out[0, :, at] = (m2_v[:, at] * inv2).astype(jnp.bfloat16)

    with span("relay3"):
        relay(PARTS - 1)
    with span("finish"):
        for h in range(PARTS):
            finish(h)
    with span("drainend"):
        for h in range(PARTS):
            keep, q1, r1, t1, u1, q2, r2, t2, u2, mine = setup(h)
            theirs = wg.at[0, pl.ds(0, chips), :, cols(h)]
            drain(theirs, rf.at[h])
            drain(theirs, sf.at[h])
            drain(wg.at[0, pl.ds(0, chips - 1), :, cols(h)], sa.at[h])
            drain(q1, sa1.at[h])
            drain(t1, sb1.at[h])
            drain(q2, sa2.at[h])
            drain(t2, sb2.at[h])
            drain(got.at[h], sp.at[h])
        for r in range(RELAYS):
            drain(xs_m.at[r, pl.ds(0, slots - per)], sm.at[r])
            drain(xs_c.at[r, pl.ds(0, slots - per)], sc.at[r])
        drain(xs_s.at[pl.ds(0, slots - per)], ss.at[0])


def _write_out(*refs):
    sem = refs[-1]
    count = (len(refs) - 1) // 2
    copies = [pltpu.make_async_copy(refs[i], refs[count + i], sem.at[i]) for i in range(count)]
    for item in copies:
        item.start()
    for item in copies:
        item.wait()


def _bytes(shape, dtype):
    return math.prod(shape) * jnp.dtype(dtype).itemsize


def on_device(send_order, master, first_code, first_scale, second_code, second_scale, grads):
    arrays = (send_order, master, first_code, first_scale, second_code, second_scale, grads)
    nd = lax.axis_size("dp")
    nt = lax.axis_size("tensor")
    slots = master.shape[1]
    width = master.shape[2]
    f32, b16, i16 = jnp.float32, jnp.bfloat16, jnp.int16
    dma = pltpu.SemaphoreType.DMA
    ny = nd // 4
    pairs = PARTS // 2
    wp = width // PARTS
    cp = width // LANES // RELAYS
    arrays = arrays[:6] + (grads.reshape(ny, 2, 2, slots, width),)
    results = (
        ((1, slots, width), f32),
        ((1, slots, width), b16),
        ((1, slots), f32),
        ((1, slots, width), b16),
        ((1, slots), f32),
        ((1, nd, slots, width), b16),
    )
    first_x, first_y = (pairs, 1, ny), (pairs, ny - 1, 2)
    then_x, then_y = (pairs, ny - 1), (pairs, 1)
    data = [(lead + (slots, wp), i16) for lead in (first_x, first_y, first_x, first_y, then_x, then_y, then_x, then_y)]
    sizes = [(lead + (1, LANES), f32) for lead in (first_x, first_y, first_x, first_y, then_x, then_y, then_x, then_y)]
    scratch = [
        ((1, slots), jnp.int32),
        ((1, slots), f32),
        ((1, slots), f32),
        ((slots, width), f32),
        ((slots, width), b16),
        ((slots, width), b16),
        ((RELAYS, slots * cp, LANES), f32),
        ((RELAYS, slots * 2 * cp, LANES), f32),
        ((RELAYS, slots, cp, LANES), i16),
        ((RELAYS, slots, 2 * cp, LANES), b16),
        ((slots, 1, LANES), f32),
        ((RELAYS, slots, cp, LANES), i16),
        ((RELAYS, slots, 2 * cp, LANES), b16),
        ((slots, 1, LANES), f32),
        ((ny, 2, slots, width), b16),
        ((PARTS, ny, 2, slots, wp), b16),
        ((pairs, ny, slots, wp), f32),
        ((pairs, 2, slots, wp), f32),
        *data,
        *sizes,
        ((slots, width), f32),
        ((slots, width), f32),
    ]
    grant = sum(_bytes(*item) for item in scratch) + sum(_bytes(*item) for item in results) + slots * 8192 + 6 * 1024 * 1024
    held = pl.pallas_call(
        functools.partial(_kernel, nd, nt, slots, width),
        out_shape=tuple(pltpu.VMEM(*item) for item in results),
        in_specs=[pl.BlockSpec(memory_space=pltpu.HBM)] * 7,
        out_specs=[pl.BlockSpec(memory_space=pltpu.VMEM)] * 6,
        scratch_shapes=[
            *(pltpu.VMEM(*item) for item in scratch),
            dma((6,)), dma((1,)),
            dma((RELAYS,)), dma((RELAYS,)), dma((1,)),
            dma((RELAYS,)), dma((RELAYS,)), dma((1,)),
            dma((PARTS,)), dma((PARTS,)),
            dma((PARTS,)), dma((PARTS,)), dma((PARTS,)), dma((PARTS,)),
            dma((PARTS,)), dma((PARTS,)), dma((PARTS,)), dma((PARTS,)),
            dma((PARTS, 2 * ny)), dma((PARTS,)), dma((PARTS,)), dma((PARTS,)),
        ],
        compiler_params=pltpu.CompilerParams(collective_id=0, has_side_effects=True, vmem_limit_bytes=grant),
        name="relayout_adam",
    )(*(pltpu.with_memory_space_constraint(item, pltpu.HBM) for item in arrays))
    return pl.pallas_call(
        _write_out,
        out_shape=tuple(jax.ShapeDtypeStruct(*item) for item in results),
        in_specs=[pl.BlockSpec(memory_space=pltpu.VMEM)] * len(results),
        out_specs=[pl.BlockSpec(memory_space=pltpu.HBM)] * len(results),
        scratch_shapes=[dma((len(results),))],
        compiler_params=pltpu.CompilerParams(vmem_limit_bytes=2 * 1024 * 1024),
        name="write_out",
    )(*(pltpu.with_memory_space_constraint(item, pltpu.VMEM) for item in held))


def solution(mesh):
    placed = (
        P(("dp", "tensor"), None),
        P(("dp", "tensor"), None, None),
        P(("dp", "tensor"), None, None),
        P(("dp", "tensor"), None),
        P(("dp", "tensor"), None, None),
        P(("dp", "tensor"), None),
        P("dp", "tensor", None, None, None),
    )
    return jax.shard_map(
        on_device,
        mesh=mesh,
        in_specs=placed,
        out_specs=(
            P(("dp", "tensor"), None, None),
            P(("dp", "tensor"), None, None),
            P(("dp", "tensor"), None),
            P(("dp", "tensor"), None, None),
            P(("dp", "tensor"), None),
            P("tensor", None, None, None),
        ),
        check_vma=False,
    )
```

time: 33.3 us -> 31.1 us (0.934)
  Pallas kernels: 32.5 us -> 30.3 us
    pallas_call x1, Pallas kernels: 31.3 us -> 29 us  [on_device(): pl.pallas_call(functools.partial(_kernel, nd, nt, slots, width), out_shap...]
where the time goes in v1:
time: 31.1 us; the launch traced here: 30.9 us
  Pallas kernels  30.3 us (97%)
  between operations  0.64 us (2%)
    pallas_call x1, Pallas kernels, on_device(): pl.pallas_call(functools.partial(_kernel, nd, nt, slots, width), out_shap...  29 us
    pallas_call x1, Pallas kernels, on_device(): pl.pallas_call(_write_out, out_shape=tuple((jax.ShapeDtypeStruct(*item) f...  1.21 us

profile of v1, /device:TPU:0, one launch (start us, length us, event | category | flops | bytes accessed | tf_op | source)
XLA Modules:
  0.0 30.9 jit_solution(1423171287558100755)
XLA Ops:
  0.6 29.0 %relayout_adam.1 = (f32[1,32,2048]{2,1,0:T(8,128)S(1)}, bf16[1,32,2048]{2,1,0:T(8,128)(2,1)S(1)}, f32[1,32]{1,0:T(1,128)S(1)}, bf16[1,32,2048]{2,1,0:T(8,128)(2,...) custom-call(s32[1,32]{1,0:T(1,128)} %order_hbm.1, f32[1,32,2048]{2,1,0:T(8,128)} %m_hbm.1, ...), custom_call_target="tpu_custom_call" | custom-call | tf_op jit(solution)/shard_map/relayout_adam/pallas_call | solution.py:471
  29.7 1.2 %write_out.1 = (f32[1,32,2048]{2,1,0:T(8,128)}, bf16[1,32,2048]{2,1,0:T(8,128)(2,1)}, f32[1,32]{1,0:T(1,128)}, bf16[1,32,2048]{2,1,0:T(8,128)(2,1)}, f32[1,32]{1,0:T(1,128)}, /*index=5*/bf16[1,8,32,2048]{3,2,1,0:T(8,128)(2,1)}) custom-call(f32[1,32,2048]{2,1,0:T(8,128)S(1)} %get-tuple-element.12.refs_0_, bf16[1,32,2048]{2,1,0:T(8,128)(2,1)S(1)} %get-tuple-element.13.refs_1_, ...), custom_call_target="tpu_custom_call" | custom-call | tf_op jit(solution)/shard_map/write_out/pallas_call | solution.py:489

commit v2 on v1

--- a/solution.py
+++ b/solution.py
@@ -25,7 +25,7 @@
             keep_x, keep_y, q1_x, q1_y, r1_x, r1_y, q2_x, q2_y, r2_x, r2_y,
             t1_x, t1_y, u1_x, u1_y, t2_x, t2_y, u2_x, u2_y, m1_v, m2_v,
             in_sem, own_sem, rm, rc, rs, sm, sc, ss, rp, sp,
-            ra1, sa1, rb1, sb1, ra2, sa2, rb2, sb2, ra, sa, rf, sf):
+            ra1, sa1, rb1, sb1, ra2, sa2, rb2, sb2, ra, sa, rf, sf, plane_in):
     n = nd * nt
     per = slots // n
     chunks = width // LANES
@@ -54,12 +54,16 @@
 
     barrier = pltpu.get_barrier_semaphore()
 
-    def greet(k, carry):
-        dst = lax.rem(me + n - k, n)
-        pl.semaphore_signal(barrier, inc=1, device_id=(dst // nt, lax.rem(dst, nt)), device_id_type=MESH)
+    def greet_column(k, carry):
+        pl.semaphore_signal(barrier, inc=1, device_id=(my_dp, lax.rem(my_t + k, nt)), device_id_type=MESH)
         return carry
 
-    lax.fori_loop(1, n, greet, 0)
+    def greet_plane(k, carry):
+        pl.semaphore_signal(barrier, inc=1, device_id=(lax.rem(my_dp + k, nd), my_t), device_id_type=MESH)
+        return carry
+
+    lax.fori_loop(1, nt, greet_column, 0)
+    lax.fori_loop(1, nd, greet_plane, 0)
 
     loads = [
         pltpu.make_async_copy(order_hbm, order_v, in_sem.at[0]),
@@ -72,9 +76,6 @@
     for item in loads:
         item.start()
 
-    load_own = pltpu.make_async_copy(g_hbm.at[:, :, my_c], own, own_sem.at[0])
-    load_own.start()
-
     def cols(h):
         return pl.ds(h * wp, wp)
 
@@ -87,6 +88,8 @@
     with span("loads"):
         for item in loads:
             item.wait()
+    load_own = pltpu.make_async_copy(g_hbm.at[:, :, my_c], own, own_sem.at[0])
+    load_own.start()
 
     eye = lax.broadcasted_iota(jnp.int32, (slots, slots), 0) == lax.broadcasted_iota(jnp.int32, (slots, slots), 1)
 
@@ -137,7 +140,13 @@
             stage(r)
 
     with span("barrier"):
-        pl.semaphore_wait(barrier, n - 1)
+        pl.semaphore_wait(barrier, nd - 1 + nt - 1)
+
+    def announce(k, carry):
+        pl.semaphore_signal(plane_in.at[my_t], inc=1, device_id=(my_dp, lax.rem(my_t + k, nt)), device_id_type=MESH)
+        return carry
+
+    lax.fori_loop(1, nt, announce, 0)
 
     def send_pairs(h):
         pltpu.make_async_remote_copy(
@@ -146,8 +155,11 @@
         ).start()
 
     def send_blocks(r):
-        for i in range(nt):
-            t = i // 2 if i % 2 == 0 else nt - 1 - i // 2
+        for t in range(nt):
+            if r == 0:
+                @pl.when(my_t != t)
+                def _(t=t):
+                    pl.semaphore_wait(plane_in.at[t], 1)
 
             def one(k, carry, t=t):
                 dp = lax.rem(my_dp + k, nd)
@@ -244,12 +256,17 @@
     with span("sendpairs"):
         for h in range(PARTS):
             send_pairs(h)
+    load_own.wait()
+
+    def first_stops():
+        for h in range(PARTS):
+            with span(f"first{h}"):
+                first_stop(h)
+
+    pl.when(2 * my_t < nt)(first_stops)
     with span("sendblocks0"):
         send_blocks(0)
-    load_own.wait()
-    for h in range(PARTS):
-        with span(f"first{h}"):
-            first_stop(h)
+    pl.when(2 * my_t >= nt)(first_stops)
     with span("sendblocks1"):
         for r in range(1, RELAYS):
             send_blocks(r)
@@ -361,7 +378,7 @@
             tops = adam(h, s1, s2, s0, tops)
         with span(f"spread{h}"):
             spread(h)
-        if h == PARTS // 2:
+        if h == PARTS // 2 - 1:
             for e in range(PARTS // 2):
                 with span(f"relay{e}"):
                     relay(e)
@@ -482,6 +499,7 @@
             dma((PARTS,)), dma((PARTS,)), dma((PARTS,)), dma((PARTS,)),
             dma((PARTS,)), dma((PARTS,)), dma((PARTS,)), dma((PARTS,)),
             dma((PARTS, 2 * ny)), dma((PARTS,)), dma((PARTS,)), dma((PARTS,)),
+            pltpu.SemaphoreType.REGULAR((nt,)),
         ],
         compiler_params=pltpu.CompilerParams(collective_id=0, has_side_effects=True, vmem_limit_bytes=grant),
         name="relayout_adam",

time: 31.1 us -> 31.4 us (level)
    pallas_call x1, Pallas kernels: 29 us -> 29.4 us  [on_device(): pl.pallas_call(functools.partial(_kernel, nd, nt, slots, width), out_shap...]
where the time goes in v2:
time: 31.4 us; the launch traced here: 31.3 us
  Pallas kernels  30.6 us (97%)
  between operations  0.64 us (2%)
    pallas_call x1, Pallas kernels, on_device(): pl.pallas_call(functools.partial(_kernel, nd, nt, slots, width), out_shap...  29.4 us
    pallas_call x1, Pallas kernels, on_device(): pl.pallas_call(_write_out, out_shape=tuple((jax.ShapeDtypeStruct(*item) f...  1.21 us

profile of v2, /device:TPU:0, one launch (start us, length us, event | category | flops | bytes accessed | tf_op | source)
XLA Modules:
  0.0 31.3 jit_solution(14383325041165531067)
XLA Ops:
  0.6 29.4 %relayout_adam.1 = (f32[1,32,2048]{2,1,0:T(8,128)S(1)}, bf16[1,32,2048]{2,1,0:T(8,128)(2,1)S(1)}, f32[1,32]{1,0:T(1,128)S(1)}, bf16[1,32,2048]{2,1,0:T(8,128)(2,...) custom-call(s32[1,32]{1,0:T(1,128)} %order_hbm.1, f32[1,32,2048]{2,1,0:T(8,128)} %m_hbm.1, ...), custom_call_target="tpu_custom_call" | custom-call | tf_op jit(solution)/shard_map/relayout_adam/pallas_call | solution.py:488
  30.1 1.2 %write_out.1 = (f32[1,32,2048]{2,1,0:T(8,128)}, bf16[1,32,2048]{2,1,0:T(8,128)(2,1)}, f32[1,32]{1,0:T(1,128)}, bf16[1,32,2048]{2,1,0:T(8,128)(2,1)}, f32[1,32]{1,0:T(1,128)}, /*index=5*/bf16[1,8,32,2048]{3,2,1,0:T(8,128)(2,1)}) custom-call(f32[1,32,2048]{2,1,0:T(8,128)S(1)} %get-tuple-element.12.refs_0_, bf16[1,32,2048]{2,1,0:T(8,128)(2,1)S(1)} %get-tuple-element.13.refs_1_, ...), custom_call_target="tpu_custom_call" | custom-call | tf_op jit(solution)/shard_map/write_out/pallas_call | solution.py:507

commit v3 on v1

--- a/solution.py
+++ b/solution.py
@@ -24,8 +24,7 @@
             xs_m, xs_c, xs_s, xr_m, xr_c, xr_s, own, got,
             keep_x, keep_y, q1_x, q1_y, r1_x, r1_y, q2_x, q2_y, r2_x, r2_y,
             t1_x, t1_y, u1_x, u1_y, t2_x, t2_y, u2_x, u2_y, m1_v, m2_v,
-            in_sem, own_sem, rm, rc, rs, sm, sc, ss, rp, sp,
-            ra1, sa1, rb1, sb1, ra2, sa2, rb2, sb2, ra, sa, rf, sf):
+            in_sem, own_sem, sent, rm, rc, rs, rp, r1st, u1st, r2nd, u2nd, ra, rf, plane_in):
     n = nd * nt
     per = slots // n
     chunks = width // LANES
@@ -54,12 +53,20 @@
 
     barrier = pltpu.get_barrier_semaphore()
 
+    def tell(sem, up):
+        where = (my_dp, my_t + 1 if up else my_t - 1)
+
+        @pl.when(my_t < nt - 1 if up else my_t > 0)
+        def _():
+            pl.semaphore_signal(sem, inc=1, device_id=where, device_id_type=MESH)
+
     def greet(k, carry):
-        dst = lax.rem(me + n - k, n)
-        pl.semaphore_signal(barrier, inc=1, device_id=(dst // nt, lax.rem(dst, nt)), device_id_type=MESH)
+        pl.semaphore_signal(barrier, inc=1, device_id=(lax.rem(my_dp + k, nd), my_t), device_id_type=MESH)
         return carry
 
-    lax.fori_loop(1, n, greet, 0)
+    tell(barrier, True)
+    tell(barrier, False)
+    lax.fori_loop(1, nd, greet, 0)
 
     loads = [
         pltpu.make_async_copy(order_hbm, order_v, in_sem.at[0]),
@@ -72,9 +79,6 @@
     for item in loads:
         item.start()
 
-    load_own = pltpu.make_async_copy(g_hbm.at[:, :, my_c], own, own_sem.at[0])
-    load_own.start()
-
     def cols(h):
         return pl.ds(h * wp, wp)
 
@@ -83,6 +87,24 @@
 
     def drain(ref, sem):
         pltpu.make_async_copy(ref, ref, sem).wait()
+
+    load_own = pltpu.make_async_copy(g_hbm.at[:, :, my_c], own, own_sem.at[0])
+
+    def send_pairs(h):
+        pltpu.make_async_remote_copy(
+            src_ref=g_hbm.at[:, :, other_c, :, cols(h)], dst_ref=got.at[h],
+            send_sem=sent.at[0], recv_sem=rp.at[h], device_id=(partner, my_t), device_id_type=MESH,
+        ).start()
+
+    with span("barrier"):
+        beside_me = jnp.where(my_t > 0, 1, 0) + jnp.where(my_t < nt - 1, 1, 0)
+        pl.semaphore_wait(barrier, nd - 1 + beside_me)
+
+    tell(plane_in.at[my_t], True)
+    tell(plane_in.at[my_t], False)
+    for h in range(PARTS):
+        send_pairs(h)
+    load_own.start()
 
     with span("loads"):
         for item in loads:
@@ -136,45 +158,48 @@
         for r in range(RELAYS):
             stage(r)
 
-    with span("barrier"):
-        pl.semaphore_wait(barrier, n - 1)
-
-    def send_pairs(h):
+    def send_block(r, t, dp):
+        dst = dp * nt + t
+        theirs, mine = pl.ds(dst * per, per), pl.ds(me * per, per)
+        where = (dp, t)
         pltpu.make_async_remote_copy(
-            src_ref=g_hbm.at[:, :, other_c, :, cols(h)], dst_ref=got.at[h],
-            send_sem=sp.at[h], recv_sem=rp.at[h], device_id=(partner, my_t), device_id_type=MESH,
+            src_ref=xs_m.at[r, theirs], dst_ref=xr_m.at[r, mine],
+            send_sem=sent.at[9], recv_sem=rm.at[r], device_id=where, device_id_type=MESH,
         ).start()
-
-    def send_blocks(r):
+        pltpu.make_async_remote_copy(
+            src_ref=xs_c.at[r, theirs], dst_ref=xr_c.at[r, mine],
+            send_sem=sent.at[10], recv_sem=rc.at[r], device_id=where, device_id_type=MESH,
+        ).start()
+        if r == 0:
+            pltpu.make_async_remote_copy(
+                src_ref=xs_s.at[theirs], dst_ref=xr_s.at[mine],
+                send_sem=sent.at[11], recv_sem=rs.at[0], device_id=where, device_id_type=MESH,
+            ).start()
+
+    early = 2 * my_t < nt
+
+    def send_blocks():
         for i in range(nt):
-            t = i // 2 if i % 2 == 0 else nt - 1 - i // 2
-
-            def one(k, carry, t=t):
-                dp = lax.rem(my_dp + k, nd)
-                dst = dp * nt + t
-                theirs, mine = pl.ds(dst * per, per), pl.ds(me * per, per)
-                where = (dp, t)
-                pltpu.make_async_remote_copy(
-                    src_ref=xs_m.at[r, theirs], dst_ref=xr_m.at[r, mine],
-                    send_sem=sm.at[r], recv_sem=rm.at[r], device_id=where, device_id_type=MESH,
-                ).start()
-                pltpu.make_async_remote_copy(
-                    src_ref=xs_c.at[r, theirs], dst_ref=xr_c.at[r, mine],
-                    send_sem=sc.at[r], recv_sem=rc.at[r], device_id=where, device_id_type=MESH,
-                ).start()
-                if r == 0:
-                    pltpu.make_async_remote_copy(
-                        src_ref=xs_s.at[theirs], dst_ref=xr_s.at[mine],
-                        send_sem=ss.at[0], recv_sem=rs.at[0], device_id=where, device_id_type=MESH,
-                    ).start()
-                return carry
-
-            lax.fori_loop(jnp.where(my_t == t, 1, 0), nd, one, 0)
+            t = jnp.where(early, i, lax.rem(nt - i, nt))
+
+            @pl.when(my_t != t)
+            def _(t=t):
+                pl.semaphore_wait(plane_in.at[t], 1)
+
+            pl.when(t < my_t)(functools.partial(tell, plane_in.at[t], True))
+            pl.when(t > my_t)(functools.partial(tell, plane_in.at[t], False))
+
+            for r in range(RELAYS):
+                def one(k, carry, r=r, t=t):
+                    send_block(r, t, lax.rem(my_dp + k, nd))
+                    return carry
+
+                lax.fori_loop(jnp.where(my_t == t, 1, 0), nd, one, 0)
         mine = pl.ds(me * per, per)
-        pltpu.make_async_copy(xs_m.at[r, mine], xr_m.at[r, mine], rm.at[r]).start()
-        pltpu.make_async_copy(xs_c.at[r, mine], xr_c.at[r, mine], rc.at[r]).start()
-        if r == 0:
-            pltpu.make_async_copy(xs_s.at[mine], xr_s.at[mine], rs.at[0]).start()
+        pltpu.make_async_copy(xs_s.at[mine], xr_s.at[mine], rs.at[0]).start()
+        for r in range(RELAYS):
+            pltpu.make_async_copy(xs_m.at[r, mine], xr_m.at[r, mine], rm.at[r]).start()
+            pltpu.make_async_copy(xs_c.at[r, mine], xr_c.at[r, mine], rc.at[r]).start()
 
     def setup(h):
         k = h // 2
@@ -208,7 +233,7 @@
     def remote(src, dst, send, recv, place):
         y, x = place
         pltpu.make_async_remote_copy(
-            src_ref=src, dst_ref=dst, send_sem=send, recv_sem=recv,
+            src_ref=src, dst_ref=dst, send_sem=sent.at[send], recv_sem=recv,
             device_id=(dp_of(y, x, my_c), my_t), device_id_type=MESH,
         ).start()
 
@@ -220,16 +245,16 @@
             place = at_first(h, a)
             for t in range(q1.shape[1]):
                 pack(pair_sum(h, *slab(h, place, t)), q1.at[a, t], t1.at[a, t])
-            remote(q1.at[a], r1.at[a], sa1.at[h], ra1.at[h], place)
-            remote(t1.at[a], u1.at[a], sb1.at[h], rb1.at[h], place)
+            remote(q1.at[a], r1.at[a], 1 + h % 2, r1st.at[h], place)
+            remote(t1.at[a], u1.at[a], 3 + h % 2, u1st.at[h], place)
         for t in range(q1.shape[1]):
             keep[t] = pair_sum(h, *slab(h, (my_y, my_x), t))
 
     def second_stop(h):
         keep, q1, r1, t1, u1, q2, r2, t2, u2, mine = setup(h)
         with span(f"waitfirst{h}"):
-            drain(r1, ra1.at[h])
-            drain(u1, rb1.at[h])
+            drain(r1, r1st.at[h])
+            drain(u1, u1st.at[h])
 
         def total(t):
             return functools.reduce(jnp.add, [unpack(r1.at[a, t], u1.at[a, t]) for a in range(r1.shape[0])], keep[t])
@@ -237,22 +262,20 @@
         for b in range(q2.shape[0]):
             y, x = at_second(h, b)
             pack(total(y if h % 2 == 0 else x), q2.at[b], t2.at[b])
-            remote(q2.at[b], r2.at[b], sa2.at[h], ra2.at[h], (y, x))
-            remote(t2.at[b], u2.at[b], sb2.at[h], rb2.at[h], (y, x))
+            remote(q2.at[b], r2.at[b], 5 + h % 2, r2nd.at[h], (y, x))
+            remote(t2.at[b], u2.at[b], 7 + h % 2, u2nd.at[h], (y, x))
         keep[mine] = total(mine)
 
-    with span("sendpairs"):
+    def first_stops():
+        load_own.wait()
         for h in range(PARTS):
-            send_pairs(h)
+            with span(f"first{h}"):
+                first_stop(h)
+
+    pl.when(early)(first_stops)
     with span("sendblocks0"):
-        send_blocks(0)
-    load_own.wait()
-    for h in range(PARTS):
-        with span(f"first{h}"):
-            first_stop(h)
-    with span("sendblocks1"):
-        for r in range(1, RELAYS):
-            send_blocks(r)
+        send_blocks()
+    pl.when(jnp.logical_not(early))(first_stops)
     for h in range(PARTS):
         with span(f"second{h}"):
             second_stop(h)
@@ -260,18 +283,24 @@
     inv_one = 1.0 / (1.0 - 0.9**STEP)
     inv_two = 1.0 / (1.0 - 0.95**STEP)
 
-    def adam(h, s1, s2, s0, tops):
+    def adam(h, tops):
         if h * RELAYS % PARTS == 0:
             r = h * RELAYS // PARTS
             with span(f"waitblocks{r}"):
+                if r == 0:
+                    drain(xr_s, rs.at[0])
                 drain(xr_m.at[r], rm.at[r])
                 drain(xr_c.at[r], rc.at[r])
             xf_m[r] = xr_m[r].astype(jnp.float32).reshape(slots * cp, LANES)
             xf_c[r] = xr_c[r].astype(jnp.float32).reshape(slots * 2 * cp, LANES)
+        scales = xr_s[:, 0, :]
+        s1 = scales[:, 0:1]
+        s2 = scales[:, LANES // 4:LANES // 4 + 1]
+        s0 = scales[:, LANES // 2:LANES // 2 + 1]
         keep, q1, r1, t1, u1, q2, r2, t2, u2, mine = setup(h)
         with span(f"waitsecond{h}"):
-            drain(r2, ra2.at[h])
-            drain(u2, rb2.at[h])
+            drain(r2, r2nd.at[h])
+            drain(u2, u2nd.at[h])
         top1, top2 = tops
         more = [as_col(u2[b, :, :slots]) for b in range(r2.shape[0])]
         for i in range(h * cq, (h + 1) * cq):
@@ -302,14 +331,14 @@
     def to_chip(h, chip, y, x):
         item = gathered(chip, h)
         pltpu.make_async_remote_copy(
-            src_ref=item, dst_ref=item, send_sem=sa.at[h], recv_sem=ra.at[h, chip],
+            src_ref=item, dst_ref=item, send_sem=sent.at[12], recv_sem=ra.at[h, chip],
             device_id=(dp_of(y, x, my_c), my_t), device_id_type=MESH,
         ).start()
 
     def to_partner(h, chip):
         item = gathered(chip, h)
         pltpu.make_async_remote_copy(
-            src_ref=item, dst_ref=item, send_sem=sf.at[h], recv_sem=rf.at[h],
+            src_ref=item, dst_ref=item, send_sem=sent.at[12], recv_sem=rf.at[0],
             device_id=(partner, my_t), device_id_type=MESH,
         ).start()
 
@@ -318,57 +347,58 @@
         pltpu.make_async_copy(item, item, ra.at[h, chip]).wait()
 
     rows_away = [row_away(away) for away in range(1, ny)]
+    beside = my_y * 2 + other_x
+    above = [y * 2 + my_x for y in rows_away]
+    corners = [y * 2 + other_x for y in rows_away]
+
+    def direct(h):
+        return 2 * h >= PARTS
 
     def spread(h):
         to_chip(h, my_chip, my_y, other_x)
         for y in rows_away:
             to_chip(h, my_chip, y, my_x)
+        if direct(h):
+            for y in rows_away:
+                to_chip(h, my_chip, y, other_x)
         to_partner(h, my_chip)
 
+    def landed(h, chip):
+        with span(f"arrive{h}"):
+            arrived(h, chip)
+        to_partner(h, chip)
+
     def relay(h):
-        if h % 2 == 0:
-            for y in rows_away:
-                chip = y * 2 + my_x
-                arrived(h, chip)
+        if direct(h):
+            for chip in [beside] + above:
+                landed(h, chip)
+        elif h % 2 == 0:
+            for chip in above:
+                with span(f"relay{h}"):
+                    arrived(h, chip)
                 to_chip(h, chip, my_y, other_x)
                 to_partner(h, chip)
+            landed(h, beside)
         else:
-            chip = my_y * 2 + other_x
-            arrived(h, chip)
+            with span(f"relay{h}"):
+                arrived(h, beside)
             for y in rows_away:
-                to_chip(h, chip, y, my_x)
-            to_partner(h, chip)
+                to_chip(h, beside, y, my_x)
+            to_partner(h, beside)
+            for chip in above:
+                landed(h, chip)
 
     def finish(h):
-        if h % 2 == 0:
-            late = [my_y * 2 + other_x]
-        else:
-            late = [y * 2 + my_x for y in rows_away]
-        for chip in late + [y * 2 + other_x for y in rows_away]:
-            arrived(h, chip)
-            to_partner(h, chip)
-
-    with span("waitscales"):
-        drain(xr_s, rs.at[0])
-    scales = xr_s[:, 0, :]
-    s1 = scales[:, 0:1]
-    s2 = scales[:, LANES // 4:LANES // 4 + 1]
-    s0 = scales[:, LANES // 2:LANES // 2 + 1]
+        for chip in corners:
+            landed(h, chip)
+
     zero = jnp.zeros((slots, LANES), jnp.float32)
     tops = (zero, zero)
     for h in range(PARTS):
         with span(f"adam{h}"):
-            tops = adam(h, s1, s2, s0, tops)
+            tops = adam(h, tops)
         with span(f"spread{h}"):
             spread(h)
-        if h == PARTS // 2:
-            for e in range(PARTS // 2):
-                with span(f"relay{e}"):
-                    relay(e)
-    with span("relay2"):
-        for h in range(PARTS // 2, PARTS - 1):
-            relay(h)
-
     with span("codes"):
         top1 = jnp.max(tops[0], axis=1, keepdims=True) + 1e-06
         top2 = jnp.max(tops[1], axis=1, keepdims=True) + 1e-06
@@ -381,27 +411,18 @@
             nc1_out[0, :, at] = (m1_v[:, at] * inv1).astype(jnp.bfloat16)
             nc2_out[0, :, at] = (m2_v[:, at] * inv2).astype(jnp.bfloat16)
 
-    with span("relay3"):
-        relay(PARTS - 1)
+    for h in range(PARTS):
+        relay(h)
     with span("finish"):
         for h in range(PARTS):
             finish(h)
     with span("drainend"):
-        for h in range(PARTS):
-            keep, q1, r1, t1, u1, q2, r2, t2, u2, mine = setup(h)
-            theirs = wg.at[0, pl.ds(0, chips), :, cols(h)]
-            drain(theirs, rf.at[h])
-            drain(theirs, sf.at[h])
-            drain(wg.at[0, pl.ds(0, chips - 1), :, cols(h)], sa.at[h])
-            drain(q1, sa1.at[h])
-            drain(t1, sb1.at[h])
-            drain(q2, sa2.at[h])
-            drain(t2, sb2.at[h])
-            drain(got.at[h], sp.at[h])
-        for r in range(RELAYS):
-            drain(xs_m.at[r, pl.ds(0, slots - per)], sm.at[r])
-            drain(xs_c.at[r, pl.ds(0, slots - per)], sc.at[r])
-        drain(xs_s.at[pl.ds(0, slots - per)], ss.at[0])
+        drain(wg.at[0, pl.ds(0, chips)], rf.at[0])
+        rest = pl.ds(0, slots - per)
+        items = (got, q1_x, q1_y, t1_x, t1_y, q2_x, q2_y, t2_x, t2_y,
+                 xs_m.at[:, rest], xs_c.at[:, rest], xs_s.at[rest], wg.at[0, pl.ds(0, 2 * chips - 1)])
+        for i, item in enumerate(items):
+            drain(item, sent.at[i])
 
 
 def _write_out(*refs):
@@ -475,13 +496,9 @@
         out_specs=[pl.BlockSpec(memory_space=pltpu.VMEM)] * 6,
         scratch_shapes=[
             *(pltpu.VMEM(*item) for item in scratch),
-            dma((6,)), dma((1,)),
-            dma((RELAYS,)), dma((RELAYS,)), dma((1,)),
-            dma((RELAYS,)), dma((RELAYS,)), dma((1,)),
-            dma((PARTS,)), dma((PARTS,)),
-            dma((PARTS,)), dma((PARTS,)), dma((PARTS,)), dma((PARTS,)),
-            dma((PARTS,)), dma((PARTS,)), dma((PARTS,)), dma((PARTS,)),
-            dma((PARTS, 2 * ny)), dma((PARTS,)), dma((PARTS,)), dma((PARTS,)),
+            dma((6,)), dma((1,)), dma((13,)), dma((RELAYS,)), dma((RELAYS,)), dma((1,)), dma((PARTS,)),
+            dma((PARTS,)), dma((PARTS,)), dma((PARTS,)), dma((PARTS,)), dma((PARTS, 2 * ny)), dma((1,)),
+            pltpu.SemaphoreType.REGULAR((nt,)),
         ],
         compiler_params=pltpu.CompilerParams(collective_id=0, has_side_effects=True, vmem_limit_bytes=grant),
         name="relayout_adam",

time: 31.1 us -> 28.2 us (0.907)
  the two profiles are of different devices: /device:TPU:0 before, /device:TPU:9 now
where the time goes in v3:
time: 28.2 us; the launch traced here: 28 us
  Pallas kernels  27.4 us (97%)
  between operations  0.64 us (2%)
    pallas_call x1, Pallas kernels, on_device(): pl.pallas_call(functools.partial(_kernel, nd, nt, slots, width), out_shap...  26.2 us
    pallas_call x1, Pallas kernels, on_device(): pl.pallas_call(_write_out, out_shape=tuple((jax.ShapeDtypeStruct(*item) f...  1.21 us

profile of v3, /device:TPU:9, one launch (start us, length us, event | category | flops | bytes accessed | tf_op | source)
XLA Modules:
  0.0 28.0 jit_solution(14295623359276391746)
XLA Ops:
  0.6 26.2 %relayout_adam.1 = (f32[1,32,2048]{2,1,0:T(8,128)S(1)}, bf16[1,32,2048]{2,1,0:T(8,128)(2,1)S(1)}, f32[1,32]{1,0:T(1,128)S(1)}, bf16[1,32,2048]{2,1,0:T(8,128)(2,...) custom-call(s32[1,32]{1,0:T(1,128)} %order_hbm.1, f32[1,32,2048]{2,1,0:T(8,128)} %m_hbm.1, ...), custom_call_target="tpu_custom_call" | custom-call | tf_op jit(solution)/shard_map/relayout_adam/pallas_call | solution.py:492
  26.8 1.2 %write_out.1 = (f32[1,32,2048]{2,1,0:T(8,128)}, bf16[1,32,2048]{2,1,0:T(8,128)(2,1)}, f32[1,32]{1,0:T(1,128)}, bf16[1,32,2048]{2,1,0:T(8,128)(2,1)}, f32[1,32]{1,0:T(1,128)}, /*index=5*/bf16[1,8,32,2048]{3,2,1,0:T(8,128)(2,1)}) custom-call(f32[1,32,2048]{2,1,0:T(8,128)S(1)} %get-tuple-element.12.refs_0_, bf16[1,32,2048]{2,1,0:T(8,128)(2,1)S(1)} %get-tuple-element.13.refs_1_, ...), custom_call_target="tpu_custom_call" | custom-call | tf_op jit(solution)/shard_map/write_out/pallas_call | solution.py:506

commit v4 on v3

--- a/solution.py
+++ b/solution.py
@@ -178,23 +178,26 @@
 
     early = 2 * my_t < nt
 
-    def send_blocks():
-        for i in range(nt):
-            t = jnp.where(early, i, lax.rem(nt - i, nt))
-
-            @pl.when(my_t != t)
-            def _(t=t):
-                pl.semaphore_wait(plane_in.at[t], 1)
-
-            pl.when(t < my_t)(functools.partial(tell, plane_in.at[t], True))
-            pl.when(t > my_t)(functools.partial(tell, plane_in.at[t], False))
-
-            for r in range(RELAYS):
-                def one(k, carry, r=r, t=t):
-                    send_block(r, t, lax.rem(my_dp + k, nd))
-                    return carry
-
-                lax.fori_loop(jnp.where(my_t == t, 1, 0), nd, one, 0)
+    def hear(t):
+        @pl.when(my_t != t)
+        def _():
+            pl.semaphore_wait(plane_in.at[t], 1)
+
+        pl.when(t < my_t)(functools.partial(tell, plane_in.at[t], True))
+        pl.when(t > my_t)(functools.partial(tell, plane_in.at[t], False))
+
+    def send_blocks(i):
+        t = jnp.where(early, i, lax.rem(nt - i, nt))
+        if i > 0:
+            hear(t)
+        for r in range(RELAYS):
+            def one(k, carry, r=r):
+                send_block(r, t, lax.rem(my_dp + k, nd))
+                return carry
+
+            lax.fori_loop(jnp.where(my_t == t, 1, 0), nd, one, 0)
+
+    def keep_blocks():
         mine = pl.ds(me * per, per)
         pltpu.make_async_copy(xs_s.at[mine], xr_s.at[mine], rs.at[0]).start()
         for r in range(RELAYS):
@@ -266,17 +269,27 @@
             remote(t2.at[b], u2.at[b], 7 + h % 2, u2nd.at[h], (y, x))
         keep[mine] = total(mine)
 
-    def first_stops():
-        load_own.wait()
-        for h in range(PARTS):
-            with span(f"first{h}"):
-                first_stop(h)
-
-    pl.when(early)(first_stops)
-    with span("sendblocks0"):
-        send_blocks()
-    pl.when(jnp.logical_not(early))(first_stops)
+    with span("hear0"):
+        hear(0)
+    load_own.wait()
     for h in range(PARTS):
+        with span(f"first{h}"):
+            first_stop(h)
+
+    def second_stops():
+        for h in range(PARTS // 2):
+            with span(f"second{h}"):
+                second_stop(h)
+
+    with span("sendblocks"):
+        for i in range(nt - 1):
+            send_blocks(i)
+        keep_blocks()
+    pl.when(early)(second_stops)
+    with span("sendlast"):
+        send_blocks(nt - 1)
+    pl.when(jnp.logical_not(early))(second_stops)
+    for h in range(PARTS // 2, PARTS):
         with span(f"second{h}"):
             second_stop(h)
 

time: 28.2 us -> 27.7 us (0.982)
  Pallas kernels: 27.4 us -> 26.8 us
    pallas_call x1, Pallas kernels: 26.2 us -> 25.6 us  [on_device(): pl.pallas_call(functools.partial(_kernel, nd, nt, slots, width), out_shap...]
where the time goes in v4:
time: 27.7 us; the launch traced here: 27.5 us
  Pallas kernels  26.8 us (97%)
  between operations  0.64 us (2%)
    pallas_call x1, Pallas kernels, on_device(): pl.pallas_call(functools.partial(_kernel, nd, nt, slots, width), out_shap...  25.6 us
    pallas_call x1, Pallas kernels, on_device(): pl.pallas_call(_write_out, out_shape=tuple((jax.ShapeDtypeStruct(*item) f...  1.21 us

profile of v4, /device:TPU:9, one launch (start us, length us, event | category | flops | bytes accessed | tf_op | source)
XLA Modules:
  0.0 27.5 jit_solution(8804548971867196233)
XLA Ops:
  0.6 25.6 %relayout_adam.1 = (f32[1,32,2048]{2,1,0:T(8,128)S(1)}, bf16[1,32,2048]{2,1,0:T(8,128)(2,1)S(1)}, f32[1,32]{1,0:T(1,128)S(1)}, bf16[1,32,2048]{2,1,0:T(8,128)(2,...) custom-call(s32[1,32]{1,0:T(1,128)} %order_hbm.1, f32[1,32,2048]{2,1,0:T(8,128)} %m_hbm.1, ...), custom_call_target="tpu_custom_call" | custom-call | tf_op jit(solution)/shard_map/relayout_adam/pallas_call | solution.py:505
  26.3 1.2 %write_out.1 = (f32[1,32,2048]{2,1,0:T(8,128)}, bf16[1,32,2048]{2,1,0:T(8,128)(2,1)}, f32[1,32]{1,0:T(1,128)}, bf16[1,32,2048]{2,1,0:T(8,128)(2,1)}, f32[1,32]{1,0:T(1,128)}, /*index=5*/bf16[1,8,32,2048]{3,2,1,0:T(8,128)(2,1)}) custom-call(f32[1,32,2048]{2,1,0:T(8,128)S(1)} %get-tuple-element.12.refs_0_, bf16[1,32,2048]{2,1,0:T(8,128)(2,1)S(1)} %get-tuple-element.13.refs_1_, ...), custom_call_target="tpu_custom_call" | custom-call | tf_op jit(solution)/shard_map/write_out/pallas_call | solution.py:519

commit v5 on v4

--- a/solution.py
+++ b/solution.py
@@ -296,7 +296,7 @@
     inv_one = 1.0 / (1.0 - 0.9**STEP)
     inv_two = 1.0 / (1.0 - 0.95**STEP)
 
-    def adam(h, tops):
+    def adam(h, scales, tops):
         if h * RELAYS % PARTS == 0:
             r = h * RELAYS // PARTS
             with span(f"waitblocks{r}"):
@@ -306,10 +306,10 @@
                 drain(xr_c.at[r], rc.at[r])
             xf_m[r] = xr_m[r].astype(jnp.float32).reshape(slots * cp, LANES)
             xf_c[r] = xr_c[r].astype(jnp.float32).reshape(slots * 2 * cp, LANES)
-        scales = xr_s[:, 0, :]
-        s1 = scales[:, 0:1]
-        s2 = scales[:, LANES // 4:LANES // 4 + 1]
-        s0 = scales[:, LANES // 2:LANES // 2 + 1]
+        if scales is None:
+            held = xr_s[:, 0, :]
+            scales = held[:, 0:1], held[:, LANES // 4:LANES // 4 + 1], held[:, LANES // 2:LANES // 2 + 1]
+        s1, s2, s0 = scales
         keep, q1, r1, t1, u1, q2, r2, t2, u2, mine = setup(h)
         with span(f"waitsecond{h}"):
             drain(r2, r2nd.at[h])
@@ -336,7 +336,7 @@
             m2_v[:, at] = two
             top1 = jnp.maximum(top1, jnp.abs(one))
             top2 = jnp.maximum(top2, jnp.abs(two))
-        return top1, top2
+        return scales, (top1, top2)
 
     def gathered(chip, h):
         return wg.at[0, chip * 2 + my_c, :, cols(h)]
@@ -406,10 +406,10 @@
             landed(h, chip)
 
     zero = jnp.zeros((slots, LANES), jnp.float32)
-    tops = (zero, zero)
+    scales, tops = None, (zero, zero)
     for h in range(PARTS):
         with span(f"adam{h}"):
-            tops = adam(h, tops)
+            scales, tops = adam(h, scales, tops)
         with span(f"spread{h}"):
             spread(h)
     with span("codes"):

time: 27.7 us -> 27.7 us (level)
  no operation moved by 1% of the time
where the time goes in v5:
time: 27.7 us; the launch traced here: 27.6 us
  Pallas kernels  26.9 us (97%)
  between operations  0.64 us (2%)
    pallas_call x1, Pallas kernels, on_device(): pl.pallas_call(functools.partial(_kernel, nd, nt, slots, width), out_shap...  25.7 us
    pallas_call x1, Pallas kernels, on_device(): pl.pallas_call(_write_out, out_shape=tuple((jax.ShapeDtypeStruct(*item) f...  1.21 us

profile of v5, /device:TPU:9, one launch (start us, length us, event | category | flops | bytes accessed | tf_op | source)
XLA Modules:
  0.0 27.6 jit_solution(12202340605848102983)
XLA Ops:
  0.6 25.7 %relayout_adam.1 = (f32[1,32,2048]{2,1,0:T(8,128)S(1)}, bf16[1,32,2048]{2,1,0:T(8,128)(2,1)S(1)}, f32[1,32]{1,0:T(1,128)S(1)}, bf16[1,32,2048]{2,1,0:T(8,128)(2,...) custom-call(s32[1,32]{1,0:T(1,128)} %order_hbm.1, f32[1,32,2048]{2,1,0:T(8,128)} %m_hbm.1, ...), custom_call_target="tpu_custom_call" | custom-call | tf_op jit(solution)/shard_map/relayout_adam/pallas_call | solution.py:505
  26.4 1.2 %write_out.1 = (f32[1,32,2048]{2,1,0:T(8,128)}, bf16[1,32,2048]{2,1,0:T(8,128)(2,1)}, f32[1,32]{1,0:T(1,128)}, bf16[1,32,2048]{2,1,0:T(8,128)(2,1)}, f32[1,32]{1,0:T(1,128)}, /*index=5*/bf16[1,8,32,2048]{3,2,1,0:T(8,128)(2,1)}) custom-call(f32[1,32,2048]{2,1,0:T(8,128)S(1)} %get-tuple-element.12.refs_0_, bf16[1,32,2048]{2,1,0:T(8,128)(2,1)S(1)} %get-tuple-element.13.refs_1_, ...), custom_call_target="tpu_custom_call" | custom-call | tf_op jit(solution)/shard_map/write_out/pallas_call | solution.py:519
